TPU v7x, 256 devices: a whole 4x4x8 slice. The times are simulated.
256 devices in a mesh: gx: 16 (over x_lo, z), ma: 16 (over y, x_hi, core).
Axes of the slice: x: 4 (x_hi: 2, x_lo: 2; x = x_hi * 2 + x_lo), y: 4, z: 8, core: 2. Of those that a mesh axis runs over, the one named last changes fastest.
Arguments:
- solution: float32 [256, 16, 8, 256], P('ma', 'gx'), may hold values from -1.2 to 1.2
- source: float32 [256, 16, 8, 256], P('ma', 'gx'), may hold values from -6 to 6
- mean_conductivity: float32 [16, 8, 256], P('gx'), may hold values from 0.5 to 2
- kl_fields: float32 [10, 16, 8, 256], P(None, 'gx'), may hold values from -0.9 to 0.9
- couplings: int32 [10, 256, 2], replicated, may hold values from 0 to 255, as said below
- mode_index: int32 [256, 10], replicated, may hold values from 0 to 3, as said below
Outputs:
- residual: float32 [256, 16, 8, 256], P('ma', 'gx')
- correction: float32 [256, 16, 8, 256], P('ma', 'gx')
Inputs may be any that keep to these rules, and one draw needn't show every extreme that they name: couplings[k, i, 0] is the mode whose multi-index is mode_index[i] plus one in variable k, couplings[k, i, 1] the mode whose multi-index is mode_index[i] minus one in variable k; where no mode has that multi-index the entry is i itself. `mode_index`: the rows are 256 distinct multi-indices of total degree at most 3 in graded order: the total degree never falls with the mode number, all multi-indices of each total degree below 3 are present, and some mode has degree 3 in one variable; the order of the variables is drawn from the seed.
All inputs are finite; a program needn't handle non-finite values.
Results may differ from a plain program's by a relative error of at most 0.000071.
Values sent between devices are 32-bit elements; how exact they have to be, the bound alone decides.
No kernel may reach another device: no remote copies, remote signals or barrier semaphores. Data moves between devices by JAX's collectives and lax.ppermute only.
A program may use at most 128 MiB of HBM per device.

v0:
```python
import jax
import jax.numpy as jnp
from jax import lax
from jax.sharding import PartitionSpec as P

STEPS = 3


def extended(array, sides, width):
    for axis, dim in sides:
        size, length = (lax.axis_size(axis), array.shape[dim])
        up = [(i, (i + 1) % size) for i in range(size)]
        down = [(j, i) for i, j in up]
        last = lax.slice_in_dim(array, length - width, length, axis=dim)
        initial = lax.slice_in_dim(array, 0, width, axis=dim)
        before = lax.ppermute(last, axis, up)
        after = lax.ppermute(initial, axis, down)
        array = jnp.concatenate([before, array, after], axis=dim)
    return array


def diffuse(coefficient, padded):
    center = coefficient[1:-1]
    values = padded[..., 1:-1, :, :]
    total = 0.5 * (center + coefficient[2:]) * (values - padded[..., 2:, :, :])
    total = total + 0.5 * (center + coefficient[:-2]) * (values - padded[..., :-2, :, :])
    for which_dim in (-2, -1):
        for offset in (-1, 1):
            total = total + 0.5 * (center + jnp.roll(center, offset, which_dim)) * (
                values - jnp.roll(values, offset, which_dim)
            )
    return total


def coupling_table(couplings, mode_index):
    modes_all = mode_index.shape[0]
    degrees = mode_index.astype(jnp.float32).T
    weight = jnp.sqrt(jnp.maximum(degrees[:, :, None], degrees[:, None, :]))
    columns = lax.broadcasted_iota(jnp.int32, (1, 1, 1, modes_all), 3)
    counted = jnp.sum((couplings[..., None] == columns).astype(jnp.float32), axis=2)
    row_ids = lax.broadcasted_iota(jnp.int32, (1, modes_all, modes_all), 1)
    col_ids = lax.broadcasted_iota(jnp.int32, (1, modes_all, modes_all), 2)
    off_diagonal = (row_ids != col_ids).astype(jnp.float32)
    return counted * weight * off_diagonal


def shards(solution, source, mean_conductivity, kl_fields, couplings, mode_index):
    modes_here = solution.shape[0]
    fields = kl_fields.shape[0]
    shape = solution.shape
    cells = shape[1] * shape[2] * shape[3]
    block_start = lax.axis_index("ma") * modes_here
    g_full = coupling_table(couplings, mode_index)
    g_rows = lax.dynamic_slice_in_dim(g_full, block_start, modes_here, 1)
    stacked = jnp.concatenate([mean_conductivity[None], kl_fields], 0)
    padded_fields = extended(stacked, (("gx", 1),), 1)
    mean_pad = padded_fields[0]
    kl_pad = padded_fields[1:]
    padded_solution = extended(solution, (("gx", 1),), 1)
    image = solution + diffuse(mean_pad, padded_solution)
    piece = lax.all_gather(padded_solution, "ma", axis=0, tiled=True)
    count = piece.shape[0]
    terms = jnp.stack([diffuse(kl_pad[field_id], piece) for field_id in range(fields)])
    terms = terms.reshape(fields, count, cells)
    coupled = jnp.einsum("kij,kjc->ic", g_rows, terms, precision=lax.Precision.HIGHEST)
    image = image + coupled.reshape(shape)
    residual = source - image
    theta = 13.0
    delta = 12.0
    sigma = theta / delta
    rho = 1.0 / sigma
    direction = residual / theta
    correction = direction
    remain = residual
    for step in range(STEPS):
        padded_direction = extended(direction, (("gx", 1),), 1)
        applied = direction + diffuse(mean_pad, padded_direction)
        remain = remain - applied
        rho_next = 1.0 / (2.0 * sigma - rho)
        direction = rho_next * rho * direction + 2.0 * rho_next / delta * remain
        correction = correction + direction
        rho = rho_next
    return (residual, correction)


def solution(mesh):
    in_specs = (
        P("ma", "gx", None, None),
        P("ma", "gx", None, None),
        P("gx", None, None),
        P(None, "gx", None, None),
        P(),
        P(),
    )
    out_specs = (P("ma", "gx", None, None), P("ma", "gx", None, None))
    return jax.shard_map(shards, mesh=mesh, in_specs=in_specs, out_specs=out_specs, check_vma=False)
```

profile of v0, /device:TPU:2, one launch (start us, length us, event | category | flops | bytes accessed | tf_op | source)
XLA Modules:
  0.0 236.9 jit_solution(6606500784124083350)
XLA Ops:
  8.2 5.9 %collective-permute-start.1 = (f32[16,1,8,256]{3,0,2,1:T(8,128)S(1)}, f32[16,1,8,256]{3,0,2,1:T(8,128)S(1)}, u32[]{:S(2)}, u32[]{:S(2)}) collective-permute-start(f32[16,1,8,256]{3,0,2,1:T(8,128)S(1)} %copy.125), channel_id=1, source_target_pairs={{16,0},{32,16},{48,32},{64,48},{80,64},{96,80},{112,96},{128,112},... | collective-permute-start | bytes 393224 | tf_op jit(solution)/shard_map/ppermute | solution.py:17
  14.1 2.8 %collective-permute-done.1 = f32[16,1,8,256]{3,0,2,1:T(8,128)S(1)} collective-permute-done((f32[16,1,8,256]{3,0,2,1:T(8,128)S(1)}, f32[16,1,8,256]{3,0,2,1:T(8,128)S(1)}, u32[]{:S(2)}, u32[]{:S(2)}) %collective-permute-start.1) | collective-permute-done | bytes 131104 | tf_op jit(solution)/shard_map/ppermute | solution.py:17
  16.9 4.3 %collective-permute-done.3 = f32[16,1,8,256]{3,0,2,1:T(8,128)S(1)} collective-permute-done((f32[16,1,8,256]{3,0,2,1:T(8,128)S(1)}, f32[16,1,8,256]{3,0,2,1:T(8,128)S(1)}, u32[]{:S(2)}, u32[]{:S(2)}) %collective-permute-start.3) | collective-permute-done | bytes 131104 | tf_op jit(solution)/shard_map/ppermute | solution.py:16
  25.6 4.0 %convert_reduce_fusion = f32[10,256,256]{2,1,0:T(8,128)} fusion(s32[10,256,2]{1,2,0:T(2,128)} %param.10), kind=kLoop, calls=%fused_computation | loop fusion | flops 3276800 | bytes 2641920 | tf_op jit(solution)/shard_map/reduce_sum | solution.py:40
  41.9 45.2 %all-gather.2.cloned.1.call-done = f32[256,3,8,256]{3,0,2,1:T(8,128)} async-done(((f32[16,3,8,256]{3,0,2,1:T(8,128)}), f32[256,3,8,256]{3,0,2,1:T(8,128)}) %all-gather.2.cloned.1.call-update) | async-done | bytes 6291472 | tf_op jit(solution)/shard_map/all_gather | solution.py:61
  87.1 4.4 %fusion.185 = (f32[256,1,8,255]{3,0,2,1:T(8,128)S(1)}, f32[256,1,8,255]{3,0,2,1:T(8,128)}) fusion(f32[256,3,8,256]{3,0,2,1:T(8,128)} %all-gather.2.cloned.1.call-done), kind=kLoop, calls=%fused_computation.401 | loop fusion | bytes 8355840 | tf_op jit(solution)/shard_map/jit(_roll_static)/slice | solution.py:30
  91.5 2.2 fusion.187
  94.6 5.4 %multiply_add_fusion = (f32[256,1,8,256]{3,0,2,1:T(8,128)}, f32[256,1,8,256]{3,0,2,1:T(8,128)S(1)}, f32[256,1,8,256]{3,0,2,1:T(8,128)S(1)}, f32[256,1,8,256]{3,0...) fusion(f32[8,256]{1,0:T(8,128)S(1)} %copy-done.93, ...), kind=kLoop, calls=%fused_computation.8 | loop fusion | flops 11010048 | bytes 29409280 | tf_op jit(solution)/shard_map/add | solution.py:29
  100.1 4.4 %multiply_add_fusion.1 = (f32[256,1,8,256]{3,0,2,1:T(8,128)}, f32[256,1,8,256]{3,0,2,1:T(8,128)}) fusion(f32[256,1,8,256]{3,0,2,1:T(8,128)S(1)} %get-tuple-element.18, f32[256,1,8,256]{3,0,2,1:T(8,128)S(1)} %get-tuple-element.17, f32[256,1,8,256]{3,0,2,1:T(8,128)S(1)} %get-tuple-element.16, f32[256,1,8,256]{3,0,2,1:T(8,128)S(1)} %get-tuple-element.15, ...), kind=kLoop, calls=%fused_computation.9 | loop fusion | flops 11534336 | bytes 16875520 | tf_op jit(solution)/shard_map/add | solution.py:29
  105.2 3.1 %copy.150 = f32[256,1,8,256]{0,3,2,1:T(8,128)} copy(f32[256,1,8,256]{3,0,2,1:T(8,128)} %get-tuple-element.20) | data formatting | bytes 4194304 | tf_op jit(solution)/shard_map/add | solution.py:29
  108.4 6.5 %multiply_add_fusion.3 = (f32[256,1,8,256]{3,0,2,1:T(8,128)}, f32[256,1,8,256]{3,0,2,1:T(8,128)}) fusion(f32[256,1,8,256]{3,0,2,1:T(8,128)} %copy-done.4, f32[256,1,8,256]{3,0,2,1:T(8,128)} %copy-done.3, f32[256,1,8,256]{3,0,2,1:T(8,128)} %copy-done.2, f32[256,1,8,256]{3,0,2,1:T(8,128)} %copy-done.1, f32[256,1,8,256]{3,0,2,1:T(8,128)} %copy-done, ...), kind=kLoop, calls=%fused_computation.11 | loop fusion | flops 11534336 | bytes 16875520 | tf_op jit(solution)/shard_map/add | solution.py:29
  115.0 3.0 %copy.144 = f32[256,1,8,256]{0,3,2,1:T(8,128)} copy(f32[256,1,8,256]{3,0,2,1:T(8,128)} %get-tuple-element.22) | data formatting | bytes 4194304 | tf_op jit(solution)/shard_map/add | solution.py:29
  118.1 6.5 %multiply_add_fusion.5 = (f32[256,1,8,256]{3,0,2,1:T(8,128)}, f32[256,1,8,256]{3,0,2,1:T(8,128)}) fusion(f32[256,1,8,256]{3,0,2,1:T(8,128)} %copy-done.4, f32[256,1,8,256]{3,0,2,1:T(8,128)} %copy-done.3, f32[256,1,8,256]{3,0,2,1:T(8,128)} %copy-done.2, f32[256,1,8,256]{3,0,2,1:T(8,128)} %copy-done.1, f32[256,1,8,256]{3,0,2,1:T(8,128)} %copy-done, ...), kind=kLoop, calls=%fused_computation.13 | loop fusion | flops 11534336 | bytes 16875520 | tf_op jit(solution)/shard_map/add | solution.py:29
  124.7 3.0 %copy.138 = f32[256,1,8,256]{0,3,2,1:T(8,128)} copy(f32[256,1,8,256]{3,0,2,1:T(8,128)} %get-tuple-element.24) | data formatting | bytes 4194304 | tf_op jit(solution)/shard_map/add | solution.py:29
  127.8 6.5 %multiply_add_fusion.7 = (f32[256,1,8,256]{3,0,2,1:T(8,128)}, f32[256,1,8,256]{3,0,2,1:T(8,128)}) fusion(f32[256,1,8,256]{3,0,2,1:T(8,128)} %copy-done.4, f32[256,1,8,256]{3,0,2,1:T(8,128)} %copy-done.3, f32[256,1,8,256]{3,0,2,1:T(8,128)} %copy-done.2, f32[256,1,8,256]{3,0,2,1:T(8,128)} %copy-done.1, f32[256,1,8,256]{3,0,2,1:T(8,128)} %copy-done, ...), kind=kLoop, calls=%fused_computation.15 | loop fusion | flops 11534336 | bytes 16875520 | tf_op jit(solution)/shard_map/add | solution.py:29
  134.3 3.0 %copy.132 = f32[256,1,8,256]{0,3,2,1:T(8,128)} copy(f32[256,1,8,256]{3,0,2,1:T(8,128)} %get-tuple-element.26) | data formatting | bytes 4194304 | tf_op jit(solution)/shard_map/add | solution.py:29
  137.3 6.7 %multiply_add_fusion.9 = f32[256,1,8,256]{3,0,2,1:T(8,128)} fusion(f32[256,1,8,256]{3,0,2,1:T(8,128)} %copy-done.4, f32[256,1,8,256]{3,0,2,1:T(8,128)} %copy-done.3, f32[256,1,8,256]{3,0,2,1:T(8,128)} %copy-done.2, f32[256,1,8,256]{3,0,2,1:T(8,128)} %copy-done.1, f32[256,1,8,256]{3,0,2,1:T(8,128)} %copy-done, f32[256,1,8,256]{3,0,2,1:T(8,128)S(1)} %get-tuple-element.13, ...), kind=kLoop, calls=%fused_computation.17 | loop fusion | flops 5767168 | bytes 14729216 | tf_op jit(solution)/shard_map/add | solution.py:29
  144.1 1.9 copy.129
  147.5 2.9 %copy.135 = f32[256,1,8,256]{0,3,2,1:T(8,128)} copy(f32[256,1,8,256]{3,0,2,1:T(8,128)} %get-tuple-element.25) | data formatting | bytes 4194304 | tf_op jit(solution)/shard_map/add | solution.py:29
  150.4 3.0 %copy.141 = f32[256,1,8,256]{0,3,2,1:T(8,128)} copy(f32[256,1,8,256]{3,0,2,1:T(8,128)} %get-tuple-element.23) | data formatting | bytes 4194304 | tf_op jit(solution)/shard_map/add | solution.py:29
  153.4 1.8 copy.147
  155.3 3.0 %copy.153 = f32[256,1,8,256]{0,3,2,1:T(8,128)} copy(f32[256,1,8,256]{3,0,2,1:T(8,128)} %get-tuple-element.19) | data formatting | bytes 4194304 | tf_op jit(solution)/shard_map/add | solution.py:29
  160.1 3.2 %constant_dynamic-update-slice_fusion.8 = f32[10,256,2048]{1,2,0:T(8,128)} fusion(f32[10,256,2048]{1,2,0:T(8,128)} %constant_dynamic-update-slice_fusion.9, f32[1,256,2048]{1,2,0:T(8,128)} %bitcast.365), kind=kLoop, calls=%fused_computation.102 | loop fusion | bytes 4194304
  181.6 20.3 %broadcast_multiply_fusion = (f32[16,1,8,256]{3,0,2,1:T(8,128)S(1)}, f32[16,1,8,256]{3,0,2,1:T(8,128)S(1)}) fusion(f32[8,256,256,10]{2,1,0,3:T(8,128)} %bitcast.361, f32[10,256,256]{2,1,0:T(8,128)} %convert_reduce_fusion, s32[]{:T(128)S(6)} %select_n.3, f32[16,256]{1,0:T(8,128)S(1)} %copy-done.31, f32[10,256]{1,0:T(8,128)S(1)} %copy-done.30, ...), kind=kOutput, calls=%fused_computation.93 | convolution fusion | flops 1007575040 | bytes 22522500 | tf_op jit(solution)/shard_map/kij,kjc->ic/dot_general | solution.py:65
  202.0 4.3 %collective-permute-start.4 = (f32[16,1,8,256]{3,0,2,1:T(8,128)S(1)}, f32[16,1,8,256]{3,0,2,1:T(8,128)S(1)}, u32[]{:S(2)}, u32[]{:S(2)}) collective-permute-start(f32[16,1,8,256]{3,0,2,1:T(8,128)S(1)} %get-tuple-element.232), channel_id=1, source_target_pairs={{16,0},{32,16},{48,32},{64,48},{80,64},{96,80},{112,96},{128,112},... | collective-permute-start | bytes 393224 | tf_op jit(solution)/shard_map/ppermute | solution.py:17
  207.1 2.3 collective-permute-done.4
  209.4 4.3 %collective-permute-done.5 = f32[16,1,8,256]{3,0,2,1:T(8,128)S(1)} collective-permute-done((f32[16,1,8,256]{3,0,2,1:T(8,128)S(1)}, f32[16,1,8,256]{3,0,2,1:T(8,128)S(1)}, u32[]{:S(2)}, u32[]{:S(2)}) %collective-permute-start.5) | collective-permute-done | bytes 131104 | tf_op jit(solution)/shard_map/ppermute | solution.py:16
  216.3 2.9 %collective-permute-done.6 = f32[16,1,8,256]{3,0,2,1:T(8,128)S(1)} collective-permute-done((f32[16,1,8,256]{3,0,2,1:T(8,128)S(1)}, f32[16,1,8,256]{3,0,2,1:T(8,128)S(1)}, u32[]{:S(2)}, u32[]{:S(2)}) %collective-permute-start.6) | collective-permute-done | bytes 131104 | tf_op jit(solution)/shard_map/ppermute | solution.py:17
  219.1 2.4 %collective-permute-done.7 = f32[16,1,8,256]{3,0,2,1:T(8,128)S(1)} collective-permute-done((f32[16,1,8,256]{3,0,2,1:T(8,128)S(1)}, f32[16,1,8,256]{3,0,2,1:T(8,128)S(1)}, u32[]{:S(2)}, u32[]{:S(2)}) %collective-permute-start.7) | collective-permute-done | bytes 131104 | tf_op jit(solution)/shard_map/ppermute | solution.py:16
  221.9 2.0 collective-permute-start.9
  224.0 2.9 %collective-permute-done.8 = f32[16,1,8,256]{3,0,2,1:T(8,128)S(1)} collective-permute-done((f32[16,1,8,256]{3,0,2,1:T(8,128)S(1)}, f32[16,1,8,256]{3,0,2,1:T(8,128)S(1)}, u32[]{:S(2)}, u32[]{:S(2)}) %collective-permute-start.8) | collective-permute-done | bytes 131104 | tf_op jit(solution)/shard_map/ppermute | solution.py:17
  226.9 2.2 collective-permute-done.9
  (285 shorter events, 45.4 us)
Async XLA Ops:
  7.2 79.9 %all-gather.2.cloned.1.call-start = ((), (), s32[]{:S(2)}) async-start(), calls=%async_computation | async-start | bytes 6684672 | tf_op jit(solution)/shard_map/all_gather | solution.py:61
  8.2 21.5 %copy-start.17 = (f32[1,8,256]{2,1,0:T(8,128)S(1)}, f32[1,8,256]{2,1,0:T(8,128)}, u32[]{:S(2)}) copy-start(f32[1,8,256]{2,1,0:T(8,128)} %param.8) | copy-start | bytes 24580
  8.2 21.4 %copy-start.16 = (f32[10,1,8,256]{3,2,1,0:T(8,128)S(1)}, f32[10,1,8,256]{3,2,1,0:T(8,128)}, u32[]{:S(2)}) copy-start(f32[10,1,8,256]{3,2,1,0:T(8,128)} %param.9) | copy-start | bytes 245764
  8.2 21.8 %copy-start.95 = (s32[256,10]{0,1:T(8,128)S(1)}, s32[256,10]{0,1:T(8,128)}, u32[]{:S(2)}) copy-start(s32[256,10]{0,1:T(8,128)} %param.11) | copy-start | bytes 30724
  8.2 8.7 %collective-permute-start.1 = (f32[16,1,8,256]{3,0,2,1:T(8,128)S(1)}, f32[16,1,8,256]{3,0,2,1:T(8,128)S(1)}, u32[]{:S(2)}, u32[]{:S(2)}) collective-permute-start(f32[16,1,8,256]{3,0,2,1:T(8,128)S(1)} %copy.125), channel_id=1, source_target_pairs={{16,0},{32,16},{48,32},{64,48},{80,64},{96,80},{112,96},{128,112},... | collective-permute-start | bytes 393224 | tf_op jit(solution)/shard_map/ppermute | solution.py:17
  14.1 7.1 %collective-permute-start.3 = (f32[16,1,8,256]{3,0,2,1:T(8,128)S(1)}, f32[16,1,8,256]{3,0,2,1:T(8,128)S(1)}, u32[]{:S(2)}, u32[]{:S(2)}) collective-permute-start(f32[16,1,8,256]{3,0,2,1:T(8,128)S(1)} %copy.125), channel_id=1, source_target_pairs={{0,16},{16,32},{32,48},{48,64},{64,80},{80,96},{96,112},{112,128},... | collective-permute-start | bytes 393224 | tf_op jit(solution)/shard_map/ppermute | solution.py:16
  22.9 11.2 %collective-permute-start = (f32[11,1,8,256]{3,2,1,0:T(8,128)S(1)}, f32[11,1,8,256]{3,2,1,0:T(8,128)S(1)}, u32[]{:S(2)}, u32[]{:S(2)}) collective-permute-start(f32[11,1,8,256]{3,2,1,0:T(8,128)S(1)} %pad_maximum_fusion.1), channel_id=1, source_target_pairs={{16,0},{32,16},{48,32},{64,48},{80,64},{96,80},{112,96},{128,112},... | collective-permute-start | bytes 270344 | tf_op jit(solution)/shard_map/ppermute | solution.py:17
  23.2 11.7 %collective-permute-start.2 = (f32[11,1,8,256]{3,2,1,0:T(8,128)S(1)}, f32[11,1,8,256]{3,2,1,0:T(8,128)S(1)}, u32[]{:S(2)}, u32[]{:S(2)}) collective-permute-start(f32[11,1,8,256]{3,2,1,0:T(8,128)S(1)} %pad_maximum_fusion.1), channel_id=1, source_target_pairs={{0,16},{16,32},{32,48},{48,64},{64,80},{80,96},{96,112},{112,128},... | collective-permute-start | bytes 270344 | tf_op jit(solution)/shard_map/ppermute | solution.py:16
  87.1 4.4 %copy-start.5 = (f32[256,3,8,256]{3,0,2,1:T(8,128)S(1)}, f32[256,3,8,256]{3,0,2,1:T(8,128)}, u32[]{:S(2)}) copy-start(f32[256,3,8,256]{3,0,2,1:T(8,128)} %all-gather.2.cloned.1.call-done) | copy-start | bytes 18874372
  94.5 5.5 %copy-start.46 = (f32[8,256]{1,0:T(8,128)S(1)}, f32[8,256]{1,0:T(8,128)}, u32[]{:S(2)}) copy-start(f32[8,256]{1,0:T(8,128)} %get-tuple-element.44) | copy-start | bytes 24580
  94.5 5.5 %copy-start.47 = (f32[8,256]{1,0:T(8,128)S(1)}, f32[8,256]{1,0:T(8,128)}, u32[]{:S(2)}) copy-start(f32[8,256]{1,0:T(8,128)} %get-tuple-element.46) | copy-start | bytes 24580
  94.5 5.5 %copy-start.50 = (f32[8,256]{1,0:T(8,128)S(1)}, f32[8,256]{1,0:T(8,128)}, u32[]{:S(2)}) copy-start(f32[8,256]{1,0:T(8,128)} %get-tuple-element.104) | copy-start | bytes 24580
  94.5 5.5 %copy-start.51 = (f32[8,256]{1,0:T(8,128)S(1)}, f32[8,256]{1,0:T(8,128)}, u32[]{:S(2)}) copy-start(f32[8,256]{1,0:T(8,128)} %get-tuple-element.112) | copy-start | bytes 24580
  94.5 5.5 %copy-start.66 = (f32[8,256]{1,0:T(8,128)S(1)}, f32[8,256]{1,0:T(8,128)}, u32[]{:S(2)}) copy-start(f32[8,256]{1,0:T(8,128)} %get-tuple-element.114) | copy-start | bytes 24580
  94.5 5.5 %copy-start.69 = (f32[8,256]{1,0:T(8,128)S(1)}, f32[8,256]{1,0:T(8,128)}, u32[]{:S(2)}) copy-start(f32[8,256]{1,0:T(8,128)} %get-tuple-element.120) | copy-start | bytes 24580
  94.5 5.5 %copy-start.77 = (f32[8,256]{1,0:T(8,128)S(1)}, f32[8,256]{1,0:T(8,128)}, u32[]{:S(2)}) copy-start(f32[8,256]{1,0:T(8,128)} %get-tuple-element.91) | copy-start | bytes 24580
  94.5 5.5 %copy-start.78 = (f32[8,256]{1,0:T(8,128)S(1)}, f32[8,256]{1,0:T(8,128)}, u32[]{:S(2)}) copy-start(f32[8,256]{1,0:T(8,128)} %get-tuple-element.92) | copy-start | bytes 24580
  94.5 5.5 %copy-start.79 = (f32[8,256]{1,0:T(8,128)S(1)}, f32[8,256]{1,0:T(8,128)}, u32[]{:S(2)}) copy-start(f32[8,256]{1,0:T(8,128)} %get-tuple-element.93) | copy-start | bytes 24580
  94.5 5.5 %copy-start.80 = (f32[8,256]{1,0:T(8,128)S(1)}, f32[8,256]{1,0:T(8,128)}, u32[]{:S(2)}) copy-start(f32[8,256]{1,0:T(8,128)} %get-tuple-element.94) | copy-start | bytes 24580
  94.5 5.5 %copy-start.87 = (f32[8,256]{1,0:T(8,128)S(1)}, f32[8,256]{1,0:T(8,128)}, u32[]{:S(2)}) copy-start(f32[8,256]{1,0:T(8,128)} %get-tuple-element.35) | copy-start | bytes 24580
  94.5 5.5 %copy-start.88 = (f32[8,256]{1,0:T(8,128)S(1)}, f32[8,256]{1,0:T(8,128)}, u32[]{:S(2)}) copy-start(f32[8,256]{1,0:T(8,128)} %get-tuple-element.37) | copy-start | bytes 24580
  99.9 4.5 %copy-start = (f32[256,1,8,256]{3,0,2,1:T(8,128)}, f32[256,1,8,256]{3,0,2,1:T(8,128)S(1)}, u32[]{:S(2)}) copy-start(f32[256,1,8,256]{3,0,2,1:T(8,128)S(1)} %get-tuple-element.14) | copy-start | bytes 6291460
  99.9 4.5 %copy-start.1 = (f32[256,1,8,256]{3,0,2,1:T(8,128)}, f32[256,1,8,256]{3,0,2,1:T(8,128)S(1)}, u32[]{:S(2)}) copy-start(f32[256,1,8,256]{3,0,2,1:T(8,128)S(1)} %get-tuple-element.15) | copy-start | bytes 6291460
  99.9 4.5 %copy-start.2 = (f32[256,1,8,256]{3,0,2,1:T(8,128)}, f32[256,1,8,256]{3,0,2,1:T(8,128)S(1)}, u32[]{:S(2)}) copy-start(f32[256,1,8,256]{3,0,2,1:T(8,128)S(1)} %get-tuple-element.16) | copy-start | bytes 6291460
  99.9 4.5 %copy-start.3 = (f32[256,1,8,256]{3,0,2,1:T(8,128)}, f32[256,1,8,256]{3,0,2,1:T(8,128)S(1)}, u32[]{:S(2)}) copy-start(f32[256,1,8,256]{3,0,2,1:T(8,128)S(1)} %get-tuple-element.17) | copy-start | bytes 6291460
  99.9 5.1 %copy-start.4 = (f32[256,1,8,256]{3,0,2,1:T(8,128)}, f32[256,1,8,256]{3,0,2,1:T(8,128)S(1)}, u32[]{:S(2)}) copy-start(f32[256,1,8,256]{3,0,2,1:T(8,128)S(1)} %get-tuple-element.18) | copy-start | bytes 6291460
  202.0 7.5 %collective-permute-start.4 = (f32[16,1,8,256]{3,0,2,1:T(8,128)S(1)}, f32[16,1,8,256]{3,0,2,1:T(8,128)S(1)}, u32[]{:S(2)}, u32[]{:S(2)}) collective-permute-start(f32[16,1,8,256]{3,0,2,1:T(8,128)S(1)} %get-tuple-element.232), channel_id=1, source_target_pairs={{16,0},{32,16},{48,32},{64,48},{80,64},{96,80},{112,96},{128,112},... | collective-permute-start | bytes 393224 | tf_op jit(solution)/shard_map/ppermute | solution.py:17
  206.3 7.5 %collective-permute-start.5 = (f32[16,1,8,256]{3,0,2,1:T(8,128)S(1)}, f32[16,1,8,256]{3,0,2,1:T(8,128)S(1)}, u32[]{:S(2)}, u32[]{:S(2)}) collective-permute-start(f32[16,1,8,256]{3,0,2,1:T(8,128)S(1)} %get-tuple-element.232), channel_id=1, source_target_pairs={{0,16},{16,32},{32,48},{48,64},{64,80},{80,96},{96,112},{112,128},... | collective-permute-start | bytes 393224 | tf_op jit(solution)/shard_map/ppermute | solution.py:16
  214.1 5.0 %collective-permute-start.6 = (f32[16,1,8,256]{3,0,2,1:T(8,128)S(1)}, f32[16,1,8,256]{3,0,2,1:T(8,128)S(1)}, u32[]{:S(2)}, u32[]{:S(2)}) collective-permute-start(f32[16,1,8,256]{3,0,2,1:T(8,128)S(1)} %get-tuple-element.10), channel_id=1, source_target_pairs={{16,0},{32,16},{48,32},{64,48},{80,64},{96,80},{112,96},{128,112},... | collective-permute-start | bytes 393224 | tf_op jit(solution)/shard_map/ppermute | solution.py:17
  214.4 7.1 %collective-permute-start.7 = (f32[16,1,8,256]{3,0,2,1:T(8,128)S(1)}, f32[16,1,8,256]{3,0,2,1:T(8,128)S(1)}, u32[]{:S(2)}, u32[]{:S(2)}) collective-permute-start(f32[16,1,8,256]{3,0,2,1:T(8,128)S(1)} %get-tuple-element.10), channel_id=1, source_target_pairs={{0,16},{16,32},{32,48},{48,64},{64,80},{80,96},{96,112},{112,128},... | collective-permute-start | bytes 393224 | tf_op jit(solution)/shard_map/ppermute | solution.py:16
  221.8 5.0 %collective-permute-start.8 = (f32[16,1,8,256]{3,0,2,1:T(8,128)S(1)}, f32[16,1,8,256]{3,0,2,1:T(8,128)S(1)}, u32[]{:S(2)}, u32[]{:S(2)}) collective-permute-start(f32[16,1,8,256]{3,0,2,1:T(8,128)S(1)} %get-tuple-element.8), channel_id=1, source_target_pairs={{16,0},{32,16},{48,32},{64,48},{80,64},{96,80},{112,96},{128,112},... | collective-permute-start | bytes 393224 | tf_op jit(solution)/shard_map/ppermute | solution.py:17
  221.9 7.2 %collective-permute-start.9 = (f32[16,1,8,256]{3,0,2,1:T(8,128)S(1)}, f32[16,1,8,256]{3,0,2,1:T(8,128)S(1)}, u32[]{:S(2)}, u32[]{:S(2)}) collective-permute-start(f32[16,1,8,256]{3,0,2,1:T(8,128)S(1)} %get-tuple-element.8), channel_id=1, source_target_pairs={{0,16},{16,32},{32,48},{48,64},{64,80},{80,96},{96,112},{112,128},... | collective-permute-start | bytes 393224 | tf_op jit(solution)/shard_map/ppermute | solution.py:16
  (75 other events, 191.4 us)
Sparse Core Ops, SparseCore 0:
  22.1 64.9 all-gather.1
where the time goes:
time: 238 us; the launch traced here: 237 us
  waiting for transfers between devices  69.2 us (29%)
  local copies, waits for them, and re-layouts  65.9 us (28%)
  other arithmetic  49.8 us (21%)
  matrix products  20.3 us (9%)
  starting transfers between devices  16.5 us (7%)
  between operations  15.2 us (6%)
    all_gather x1, waiting for transfers between devices, shards(): piece = lax.all_gather(padded_solution, 'ma', axis=0, tiled=True)  45.2 us
    add x6, other arithmetic, diffuse(): total + 0.5 * (center + jnp.roll(center, offset, which_dim)) * (values -...  36 us
    add x10, local copies, waits for them, and re-layouts, diffuse(): total + 0.5 * (center + jnp.roll(center, offset, which_dim)) * (values -...  26.6 us
    unnamed x204, local copies, waits for them, and re-layouts  24.9 us
    dot_general x1, matrix products, shards(): jnp.einsum('kij,kjc->ic', g_rows, terms, precision=lax.Precision.HIGHEST)  20.3 us
    ppermute x5, waiting for transfers between devices, extended(): before = lax.ppermute(last, axis, up)  13.2 us
    ppermute x5, starting transfers between devices, extended(): after = lax.ppermute(initial, axis, down)  10.9 us
    ppermute x5, waiting for transfers between devices, extended(): after = lax.ppermute(initial, axis, down)  10.8 us
  transfers between devices with their start and end apart: 11, of which 9 were waited for; matrix products, arithmetic and copies ran while one was open for 8% of the time, Pallas kernels for 0%

commit v1 on v0

--- a/solution.py
+++ b/solution.py
@@ -58,7 +58,8 @@
     kl_pad = padded_fields[1:]
     padded_solution = extended(solution, (("gx", 1),), 1)
     image = solution + diffuse(mean_pad, padded_solution)
-    piece = lax.all_gather(padded_solution, "ma", axis=0, tiled=True)
+    outgoing = jnp.stack([padded_solution] * lax.axis_size("ma"))
+    piece = jnp.concatenate(lax.all_to_all(outgoing, "ma", 0, 0), axis=0)
     count = piece.shape[0]
     terms = jnp.stack([diffuse(kl_pad[field_id], piece) for field_id in range(fields)])
     terms = terms.reshape(fields, count, cells)

time: 238 us -> 256 us (1.076)
  waiting for transfers between devices: 69.2 us -> 84.3 us
  between operations: 15.2 us -> 1.95 us
  local copies, waits for them, and re-layouts: 65.9 us -> 77.2 us
  starting transfers between devices: 16.5 us -> 25.5 us
  other arithmetic: 49.8 us -> 45.5 us
    all_to_all x0 -> x1, waiting for transfers between devices: none -> 67.9 us  [shards(): piece = jnp.concatenate(lax.all_to_all(outgoing, 'ma', 0, 0), axis=0)]
    all_gather x1 -> x0, waiting for transfers between devices: 45.2 us -> none  [shards(): piece = lax.all_gather(padded_solution, 'ma', axis=0, tiled=True)]
    another operation x1 -> x11, local copies, waits for them, and re-layouts: 1.5 us -> 28.3 us  [shards(): jnp.stack([diffuse(kl_pad[field_id], piece) for field_id in range(fields)])]
    add x10 -> x0, local copies, waits for them, and re-layouts: 26.6 us -> none  [diffuse(): total + 0.5 * (center + jnp.roll(center, offset, which_dim)) * (values -...]
    all_to_all x0 -> x1, starting transfers between devices: none -> 6.49 us  [shards(): piece = jnp.concatenate(lax.all_to_all(outgoing, 'ma', 0, 0), axis=0)]
    ppermute x5, waiting for transfers between devices: 13.2 us -> 8.96 us  [extended(): before = lax.ppermute(last, axis, up)]
    ppermute x5, starting transfers between devices: 10.9 us -> 15 us  [extended(): after = lax.ppermute(initial, axis, down)]
    ppermute x5, waiting for transfers between devices: 10.8 us -> 7.4 us  [extended(): after = lax.ppermute(initial, axis, down)]
  transfers between devices with their start and end apart: 11 -> 11, of which waited for: 9 -> 7; matrix products, arithmetic and copies ran while one was open for 8% -> 8% of each run, Pallas kernels for 0% -> 0%
where the time goes in v1:
time: 256 us; the launch traced here: 255 us
  waiting for transfers between devices  84.3 us (33%)
  local copies, waits for them, and re-layouts  77.2 us (30%)
  other arithmetic  45.5 us (18%)
  starting transfers between devices  25.5 us (10%)
  matrix products  20.3 us (8%)
    all_to_all x1, waiting for transfers between devices, shards(): piece = jnp.concatenate(lax.all_to_all(outgoing, 'ma', 0, 0), axis=0)  67.9 us
    add x6, other arithmetic, diffuse(): total + 0.5 * (center + jnp.roll(center, offset, which_dim)) * (values -...  33.7 us
    another operation x11, local copies, waits for them, and re-layouts, shards(): jnp.stack([diffuse(kl_pad[field_id], piece) for field_id in range(fields)])  28.3 us
    unnamed x204, local copies, waits for them, and re-layouts  25.6 us
    dot_general x1, matrix products, shards(): jnp.einsum('kij,kjc->ic', g_rows, terms, precision=lax.Precision.HIGHEST)  20.3 us
    ppermute x5, starting transfers between devices, extended(): after = lax.ppermute(initial, axis, down)  15 us
    slice x20, local copies, waits for them, and re-layouts, diffuse(): jnp.roll(values, offset, which_dim)  13.6 us
    ppermute x5, waiting for transfers between devices, extended(): before = lax.ppermute(last, axis, up)  8.96 us
  transfers between devices with their start and end apart: 11, of which 7 were waited for; matrix products, arithmetic and copies ran while one was open for 8% of the time, Pallas kernels for 0%

profile of v1, /device:TPU:2, one launch (start us, length us, event | category | flops | bytes accessed | tf_op | source)
XLA Modules:
  0.0 254.7 jit_solution(9514024273658457474)
XLA Ops:
  1.6 5.8 %collective-permute-start = (f32[11,1,8,256]{3,2,1,0:T(8,128)S(1)}, f32[11,1,8,256]{3,2,1,0:T(8,128)S(1)}, u32[]{:S(2)}, u32[]{:S(2)}) collective-permute-start(f32[11,1,8,256]{3,2,1,0:T(8,128)S(1)} %pad_maximum_fusion.1), channel_id=1, source_target_pairs={{16,0},{32,16},{48,32},{64,48},{80,64},{96,80},{112,96},{128,112},... | collective-permute-start | bytes 270344 | tf_op jit(solution)/shard_map/ppermute | solution.py:17
  8.3 4.2 %collective-permute-start.1 = (f32[16,1,8,256]{3,0,2,1:T(8,128)S(1)}, f32[16,1,8,256]{3,0,2,1:T(8,128)S(1)}, u32[]{:S(2)}, u32[]{:S(2)}) collective-permute-start(f32[16,1,8,256]{3,0,2,1:T(8,128)S(1)} %copy.173), channel_id=1, source_target_pairs={{16,0},{32,16},{48,32},{64,48},{80,64},{96,80},{112,96},{128,112},... | collective-permute-start | bytes 393224 | tf_op jit(solution)/shard_map/ppermute | solution.py:17
  19.4 2.7 %convert_reduce_fusion = f32[10,256,256]{2,1,0:T(8,128)} fusion(s32[10,256,2]{1,2,0:T(2,128)S(1)} %copy-done.94), kind=kLoop, calls=%fused_computation | loop fusion | flops 3276800 | bytes 2641920 | tf_op jit(solution)/shard_map/reduce_sum | solution.py:40
  25.8 3.3 %stack.24 = f32[16,16,3,8,256]{4,3,2,1,0:T(8,128)} broadcast(f32[16,3,8,256]{3,2,1,0:T(8,128)S(1)} %copy.175), dimensions={1,2,3,4} | broadcast | bytes 6684672 | tf_op jit(solution)/shard_map/stack | solution.py:61
  29.1 6.5 %all-to-all-start = ((f32[16,16,3,8,256]{4,3,2,1,0:T(8,128)}), f32[16,16,3,8,256]{4,3,2,1,0:T(8,128)}, u32[]{:S(2)}, u32[]{:S(2)}) async-start(f32[16,16,3,8,256]{4,3,2,1,0:T(8,128)} %stack.24), calls=%async_computation | async-start | bytes 12582912 | tf_op jit(solution)/shard_map/all_to_all | solution.py:62
  42.0 67.9 %all-to-all-done = f32[16,16,3,8,256]{4,3,2,1,0:T(8,128)} async-done(((f32[16,16,3,8,256]{4,3,2,1,0:T(8,128)}), f32[16,16,3,8,256]{4,3,2,1,0:T(8,128)}, u32[]{:S(2)}, u32[]{:S(2)}) %all-to-all-start) | async-done | bytes 6291488 | tf_op jit(solution)/shard_map/all_to_all | solution.py:62
  109.9 3.0 %fusion.185 = (f32[256,1,8,255]{3,2,1,0:T(8,128)S(1)}, f32[256,1,8,255]{3,2,1,0:T(8,128)S(1)}) fusion(f32[256,3,8,256]{3,2,1,0:T(8,128)} %bitcast.15), kind=kLoop, calls=%fused_computation.401 | loop fusion | bytes 8355840 | tf_op jit(solution)/shard_map/jit(_roll_static)/slice | solution.py:30
  112.9 2.6 %fusion.187 = (f32[256,1,7,256]{3,2,1,0:T(8,128)S(1)}, f32[256,1,7,256]{3,2,1,0:T(8,128)S(1)}) fusion(f32[256,3,8,256]{3,2,1,0:T(8,128)} %bitcast.15), kind=kLoop, calls=%fused_computation.403 | loop fusion | bytes 7340032 | tf_op jit(solution)/shard_map/jit(_roll_static)/slice | solution.py:30
  117.5 2.7 %fusion.186 = (f32[256,1,1,256]{3,2,1,0:T(1,128)S(1)}, f32[256,1,1,256]{3,2,1,0:T(1,128)S(1)}) fusion(f32[256,3,8,256]{3,2,1,0:T(8,128)} %bitcast.15), kind=kLoop, calls=%fused_computation.402 | loop fusion | bytes 1048576 | tf_op jit(solution)/shard_map/jit(_roll_static)/slice | solution.py:30
  120.3 5.4 %multiply_add_fusion = (f32[256,1,8,256]{3,2,1,0:T(8,128)}, f32[256,1,8,256]{3,2,1,0:T(8,128)S(1)}, f32[256,1,8,256]{3,2,1,0:T(8,128)S(1)}, f32[256,1,8,256]{3,2...) fusion(f32[8,256]{1,0:T(8,128)S(1)} %copy-done.78, ...), kind=kLoop, calls=%fused_computation.8 | loop fusion | flops 11010048 | bytes 29409280 | tf_op jit(solution)/shard_map/add | solution.py:29
  125.9 3.5 %multiply_add_fusion.1 = (f32[256,1,8,256]{3,2,1,0:T(8,128)}, f32[256,1,8,256]{3,2,1,0:T(8,128)}) fusion(f32[256,1,8,256]{3,2,1,0:T(8,128)S(1)} %get-tuple-element.20, f32[256,1,8,256]{3,2,1,0:T(8,128)S(1)} %get-tuple-element.19, f32[256,1,8,256]{3,2,1,0:T(8,128)S(1)} %get-tuple-element.18, f32[256,1,8,256]{3,2,1,0:T(8,128)S(1)} %get-tuple-element.17, ...), kind=kLoop, calls=%fused_computation.9 | loop fusion | flops 11534336 | bytes 16875520 | tf_op jit(solution)/shard_map/add | solution.py:29
  131.2 3.1 %copy.218 = f32[256,1,8,256]{0,3,2,1:T(8,128)} copy(f32[256,1,8,256]{3,2,1,0:T(8,128)} %get-tuple-element.22) | data formatting | bytes 4194304 | tf_op jit(solution)/shard_map/stack | solution.py:64
  134.4 6.2 %multiply_add_fusion.3 = (f32[256,1,8,256]{3,2,1,0:T(8,128)}, f32[256,1,8,256]{3,2,1,0:T(8,128)}) fusion(f32[256,1,8,256]{3,2,1,0:T(8,128)} %copy-done.4, f32[256,1,8,256]{3,2,1,0:T(8,128)} %copy-done.3, f32[256,1,8,256]{3,2,1,0:T(8,128)} %copy-done.2, f32[256,1,8,256]{3,2,1,0:T(8,128)} %copy-done.1, f32[256,1,8,256]{3,2,1,0:T(8,128)} %copy-done, ...), kind=kLoop, calls=%fused_computation.11 | loop fusion | flops 11534336 | bytes 16875520 | tf_op jit(solution)/shard_map/add | solution.py:29
  140.7 3.0 %copy.216 = f32[256,1,8,256]{0,3,2,1:T(8,128)} copy(f32[256,1,8,256]{3,2,1,0:T(8,128)} %get-tuple-element.24) | data formatting | bytes 4194304 | tf_op jit(solution)/shard_map/stack | solution.py:64
  143.8 6.2 %multiply_add_fusion.5 = (f32[256,1,8,256]{3,2,1,0:T(8,128)}, f32[256,1,8,256]{3,2,1,0:T(8,128)}) fusion(f32[256,1,8,256]{3,2,1,0:T(8,128)} %copy-done.4, f32[256,1,8,256]{3,2,1,0:T(8,128)} %copy-done.3, f32[256,1,8,256]{3,2,1,0:T(8,128)} %copy-done.2, f32[256,1,8,256]{3,2,1,0:T(8,128)} %copy-done.1, f32[256,1,8,256]{3,2,1,0:T(8,128)} %copy-done, ...), kind=kLoop, calls=%fused_computation.13 | loop fusion | flops 11534336 | bytes 16875520 | tf_op jit(solution)/shard_map/add | solution.py:29
  150.1 3.0 %copy.214 = f32[256,1,8,256]{0,3,2,1:T(8,128)} copy(f32[256,1,8,256]{3,2,1,0:T(8,128)} %get-tuple-element.26) | data formatting | bytes 4194304 | tf_op jit(solution)/shard_map/stack | solution.py:64
  153.2 6.2 %multiply_add_fusion.7 = (f32[256,1,8,256]{3,2,1,0:T(8,128)}, f32[256,1,8,256]{3,2,1,0:T(8,128)}) fusion(f32[256,1,8,256]{3,2,1,0:T(8,128)} %copy-done.4, f32[256,1,8,256]{3,2,1,0:T(8,128)} %copy-done.3, f32[256,1,8,256]{3,2,1,0:T(8,128)} %copy-done.2, f32[256,1,8,256]{3,2,1,0:T(8,128)} %copy-done.1, f32[256,1,8,256]{3,2,1,0:T(8,128)} %copy-done, ...), kind=kLoop, calls=%fused_computation.15 | loop fusion | flops 11534336 | bytes 16875520 | tf_op jit(solution)/shard_map/add | solution.py:29
  159.5 3.0 %copy.212 = f32[256,1,8,256]{0,3,2,1:T(8,128)} copy(f32[256,1,8,256]{3,2,1,0:T(8,128)} %get-tuple-element.28) | data formatting | bytes 4194304 | tf_op jit(solution)/shard_map/stack | solution.py:64
  162.5 6.2 %multiply_add_fusion.9 = f32[256,1,8,256]{3,2,1,0:T(8,128)} fusion(f32[256,1,8,256]{3,2,1,0:T(8,128)} %copy-done.4, f32[256,1,8,256]{3,2,1,0:T(8,128)} %copy-done.3, f32[256,1,8,256]{3,2,1,0:T(8,128)} %copy-done.2, f32[256,1,8,256]{3,2,1,0:T(8,128)} %copy-done.1, f32[256,1,8,256]{3,2,1,0:T(8,128)} %copy-done, f32[256,1,8,256]{3,2,1,0:T(8,128)S(1)} %get-tuple-element.15, ...), kind=kLoop, calls=%fused_computation.17 | loop fusion | flops 5767168 | bytes 14729216 | tf_op jit(solution)/shard_map/add | solution.py:29
  172.1 3.0 %copy.213 = f32[256,1,8,256]{0,3,2,1:T(8,128)} copy(f32[256,1,8,256]{3,2,1,0:T(8,128)} %get-tuple-element.27) | data formatting | bytes 4194304 | tf_op jit(solution)/shard_map/stack | solution.py:64
  175.1 3.1 %copy.215 = f32[256,1,8,256]{0,3,2,1:T(8,128)} copy(f32[256,1,8,256]{3,2,1,0:T(8,128)} %get-tuple-element.25) | data formatting | bytes 4194304 | tf_op jit(solution)/shard_map/stack | solution.py:64
  180.0 3.1 %copy.219 = f32[256,1,8,256]{0,3,2,1:T(8,128)} copy(f32[256,1,8,256]{3,2,1,0:T(8,128)} %get-tuple-element.21) | data formatting | bytes 4194304 | tf_op jit(solution)/shard_map/stack | solution.py:64
  184.9 3.2 %constant_dynamic-update-slice_fusion.8 = f32[10,256,2048]{1,2,0:T(8,128)} fusion(f32[10,256,2048]{1,2,0:T(8,128)} %constant_dynamic-update-slice_fusion.9, f32[1,256,2048]{1,2,0:T(8,128)} %bitcast.366), kind=kLoop, calls=%fused_computation.102 | loop fusion | bytes 4194304
  206.3 20.3 %broadcast_multiply_fusion = (f32[16,1,8,256]{3,0,2,1:T(8,128)S(1)}, f32[16,1,8,256]{3,0,2,1:T(8,128)S(1)}) fusion(f32[8,256,256,10]{2,1,0,3:T(8,128)} %bitcast.362, f32[10,256,256]{2,1,0:T(8,128)} %convert_reduce_fusion, s32[]{:T(128)S(6)} %select_n.3, f32[16,256]{1,0:T(8,128)S(1)} %copy-done.30, f32[10,256]{1,0:T(8,128)S(1)} %copy-done.29, ...), kind=kOutput, calls=%fused_computation.93 | convolution fusion | flops 1007575040 | bytes 22522500 | tf_op jit(solution)/shard_map/kij,kjc->ic/dot_general | solution.py:66
  226.8 4.8 %collective-permute-start.4 = (f32[16,1,8,256]{3,0,2,1:T(8,128)S(1)}, f32[16,1,8,256]{3,0,2,1:T(8,128)S(1)}, u32[]{:S(2)}, u32[]{:S(2)}) collective-permute-start(f32[16,1,8,256]{3,0,2,1:T(8,128)S(1)} %get-tuple-element.234), channel_id=1, source_target_pairs={{16,0},{32,16},{48,32},{64,48},{80,64},{96,80},{112,96},{128,112},... | collective-permute-start | bytes 393224 | tf_op jit(solution)/shard_map/ppermute | solution.py:17
  234.1 4.6 %collective-permute-done.5 = f32[16,1,8,256]{3,0,2,1:T(8,128)S(1)} collective-permute-done((f32[16,1,8,256]{3,0,2,1:T(8,128)S(1)}, f32[16,1,8,256]{3,0,2,1:T(8,128)S(1)}, u32[]{:S(2)}, u32[]{:S(2)}) %collective-permute-start.5) | collective-permute-done | bytes 131104 | tf_op jit(solution)/shard_map/ppermute | solution.py:16
  239.1 2.0 collective-permute-start.7
  241.2 2.9 %collective-permute-done.6 = f32[16,1,8,256]{3,0,2,1:T(8,128)S(1)} collective-permute-done((f32[16,1,8,256]{3,0,2,1:T(8,128)S(1)}, f32[16,1,8,256]{3,0,2,1:T(8,128)S(1)}, u32[]{:S(2)}, u32[]{:S(2)}) %collective-permute-start.6) | collective-permute-done | bytes 131104 | tf_op jit(solution)/shard_map/ppermute | solution.py:17
  244.0 2.2 collective-permute-done.7
  246.6 2.0 collective-permute-start.9
  248.7 2.9 %collective-permute-done.8 = f32[16,1,8,256]{3,0,2,1:T(8,128)S(1)} collective-permute-done((f32[16,1,8,256]{3,0,2,1:T(8,128)S(1)}, f32[16,1,8,256]{3,0,2,1:T(8,128)S(1)}, u32[]{:S(2)}, u32[]{:S(2)}) %collective-permute-start.8) | collective-permute-done | bytes 131104 | tf_op jit(solution)/shard_map/ppermute | solution.py:17
  251.6 2.2 collective-permute-done.9
  (286 shorter events, 52.2 us)
Async XLA Ops:
  0.6 18.8 %copy-start.95 = (s32[256,10]{0,1:T(8,128)S(1)}, s32[256,10]{0,1:T(8,128)}, u32[]{:S(2)}) copy-start(s32[256,10]{0,1:T(8,128)} %param.11) | copy-start | bytes 30724
  0.6 18.8 %copy-start.94 = (s32[10,256,2]{1,2,0:T(2,128)S(1)}, s32[10,256,2]{1,2,0:T(2,128)}, u32[]{:S(2)}) copy-start(s32[10,256,2]{1,2,0:T(2,128)} %param.10) | copy-start | bytes 61444
  1.6 22.6 %collective-permute-start = (f32[11,1,8,256]{3,2,1,0:T(8,128)S(1)}, f32[11,1,8,256]{3,2,1,0:T(8,128)S(1)}, u32[]{:S(2)}, u32[]{:S(2)}) collective-permute-start(f32[11,1,8,256]{3,2,1,0:T(8,128)S(1)} %pad_maximum_fusion.1), channel_id=1, source_target_pairs={{16,0},{32,16},{48,32},{64,48},{80,64},{96,80},{112,96},{128,112},... | collective-permute-start | bytes 270344 | tf_op jit(solution)/shard_map/ppermute | solution.py:17
  7.4 17.5 %collective-permute-start.2 = (f32[11,1,8,256]{3,2,1,0:T(8,128)S(1)}, f32[11,1,8,256]{3,2,1,0:T(8,128)S(1)}, u32[]{:S(2)}, u32[]{:S(2)}) collective-permute-start(f32[11,1,8,256]{3,2,1,0:T(8,128)S(1)} %pad_maximum_fusion.1), channel_id=1, source_target_pairs={{0,16},{16,32},{32,48},{48,64},{64,80},{80,96},{96,112},{112,128},... | collective-permute-start | bytes 270344 | tf_op jit(solution)/shard_map/ppermute | solution.py:16
  8.3 17.2 %collective-permute-start.1 = (f32[16,1,8,256]{3,0,2,1:T(8,128)S(1)}, f32[16,1,8,256]{3,0,2,1:T(8,128)S(1)}, u32[]{:S(2)}, u32[]{:S(2)}) collective-permute-start(f32[16,1,8,256]{3,0,2,1:T(8,128)S(1)} %copy.173), channel_id=1, source_target_pairs={{16,0},{32,16},{48,32},{64,48},{80,64},{96,80},{112,96},{128,112},... | collective-permute-start | bytes 393224 | tf_op jit(solution)/shard_map/ppermute | solution.py:17
  12.5 13.0 %collective-permute-start.3 = (f32[16,1,8,256]{3,0,2,1:T(8,128)S(1)}, f32[16,1,8,256]{3,0,2,1:T(8,128)S(1)}, u32[]{:S(2)}, u32[]{:S(2)}) collective-permute-start(f32[16,1,8,256]{3,0,2,1:T(8,128)S(1)} %copy.173), channel_id=1, source_target_pairs={{0,16},{16,32},{32,48},{48,64},{64,80},{80,96},{96,112},{112,128},... | collective-permute-start | bytes 393224 | tf_op jit(solution)/shard_map/ppermute | solution.py:16
  16.6 6.2 %copy-start.16 = (f32[1,8,256]{2,1,0:T(8,128)S(1)}, f32[1,8,256]{2,1,0:T(8,128)}, u32[]{:S(2)}) copy-start(f32[1,8,256]{2,1,0:T(8,128)} %param.8) | copy-start | bytes 24580
  16.6 7.5 %copy-start.15 = (f32[10,1,8,256]{3,2,1,0:T(8,128)S(1)}, f32[10,1,8,256]{3,2,1,0:T(8,128)}, u32[]{:S(2)}) copy-start(f32[10,1,8,256]{3,2,1,0:T(8,128)} %param.9) | copy-start | bytes 245764
  19.4 6.4 %copy-start.28 = (f32[10,256]{1,0:T(8,128)}, f32[10,256]{1,0:T(8,128)S(1)}, u32[]{:S(2)}) copy-start(f32[10,256]{1,0:T(8,128)S(1)} %convert_bitcast_fusion) | copy-start | bytes 30724
  29.1 80.8 %all-to-all-start = ((f32[16,16,3,8,256]{4,3,2,1,0:T(8,128)}), f32[16,16,3,8,256]{4,3,2,1,0:T(8,128)}, u32[]{:S(2)}, u32[]{:S(2)}) async-start(f32[16,16,3,8,256]{4,3,2,1,0:T(8,128)} %stack.24), calls=%async_computation | async-start | bytes 12582912 | tf_op jit(solution)/shard_map/all_to_all | solution.py:62
  115.5 4.7 %copy-start.47 = (f32[8,256]{1,0:T(8,128)S(1)}, f32[8,256]{1,0:T(8,128)}, u32[]{:S(2)}) copy-start(f32[8,256]{1,0:T(8,128)} %get-tuple-element.47) | copy-start | bytes 24580
  115.5 4.7 %copy-start.66 = (f32[8,256]{1,0:T(8,128)S(1)}, f32[8,256]{1,0:T(8,128)}, u32[]{:S(2)}) copy-start(f32[8,256]{1,0:T(8,128)} %get-tuple-element.138) | copy-start | bytes 24580
  115.5 4.7 %copy-start.67 = (f32[8,256]{1,0:T(8,128)S(1)}, f32[8,256]{1,0:T(8,128)}, u32[]{:S(2)}) copy-start(f32[8,256]{1,0:T(8,128)} %get-tuple-element.139) | copy-start | bytes 24580
  120.2 5.5 %copy-start.45 = (f32[8,256]{1,0:T(8,128)S(1)}, f32[8,256]{1,0:T(8,128)}, u32[]{:S(2)}) copy-start(f32[8,256]{1,0:T(8,128)} %get-tuple-element.46) | copy-start | bytes 24580
  120.2 5.5 %copy-start.46 = (f32[8,256]{1,0:T(8,128)S(1)}, f32[8,256]{1,0:T(8,128)}, u32[]{:S(2)}) copy-start(f32[8,256]{1,0:T(8,128)} %get-tuple-element.48) | copy-start | bytes 24580
  120.2 5.5 %copy-start.50 = (f32[8,256]{1,0:T(8,128)S(1)}, f32[8,256]{1,0:T(8,128)}, u32[]{:S(2)}) copy-start(f32[8,256]{1,0:T(8,128)} %get-tuple-element.106) | copy-start | bytes 24580
  120.3 5.5 %copy-start.51 = (f32[8,256]{1,0:T(8,128)S(1)}, f32[8,256]{1,0:T(8,128)}, u32[]{:S(2)}) copy-start(f32[8,256]{1,0:T(8,128)} %get-tuple-element.114) | copy-start | bytes 24580
  120.3 5.5 %copy-start.68 = (f32[8,256]{1,0:T(8,128)S(1)}, f32[8,256]{1,0:T(8,128)}, u32[]{:S(2)}) copy-start(f32[8,256]{1,0:T(8,128)} %get-tuple-element.116) | copy-start | bytes 24580
  120.3 5.5 %copy-start.71 = (f32[8,256]{1,0:T(8,128)S(1)}, f32[8,256]{1,0:T(8,128)}, u32[]{:S(2)}) copy-start(f32[8,256]{1,0:T(8,128)} %get-tuple-element.122) | copy-start | bytes 24580
  120.3 5.5 %copy-start.81 = (f32[8,256]{1,0:T(8,128)S(1)}, f32[8,256]{1,0:T(8,128)}, u32[]{:S(2)}) copy-start(f32[8,256]{1,0:T(8,128)} %get-tuple-element.93) | copy-start | bytes 24580
  120.3 5.5 %copy-start.82 = (f32[8,256]{1,0:T(8,128)S(1)}, f32[8,256]{1,0:T(8,128)}, u32[]{:S(2)}) copy-start(f32[8,256]{1,0:T(8,128)} %get-tuple-element.94) | copy-start | bytes 24580
  120.3 5.5 %copy-start.83 = (f32[8,256]{1,0:T(8,128)S(1)}, f32[8,256]{1,0:T(8,128)}, u32[]{:S(2)}) copy-start(f32[8,256]{1,0:T(8,128)} %get-tuple-element.95) | copy-start | bytes 24580
  120.3 5.5 %copy-start.84 = (f32[8,256]{1,0:T(8,128)S(1)}, f32[8,256]{1,0:T(8,128)}, u32[]{:S(2)}) copy-start(f32[8,256]{1,0:T(8,128)} %get-tuple-element.96) | copy-start | bytes 24580
  120.3 5.5 %copy-start.91 = (f32[8,256]{1,0:T(8,128)S(1)}, f32[8,256]{1,0:T(8,128)}, u32[]{:S(2)}) copy-start(f32[8,256]{1,0:T(8,128)} %get-tuple-element.37) | copy-start | bytes 24580
  120.3 5.5 %copy-start.92 = (f32[8,256]{1,0:T(8,128)S(1)}, f32[8,256]{1,0:T(8,128)}, u32[]{:S(2)}) copy-start(f32[8,256]{1,0:T(8,128)} %get-tuple-element.39) | copy-start | bytes 24580
  125.8 5.3 %copy-start.4 = (f32[256,1,8,256]{3,2,1,0:T(8,128)}, f32[256,1,8,256]{3,2,1,0:T(8,128)S(1)}, u32[]{:S(2)}) copy-start(f32[256,1,8,256]{3,2,1,0:T(8,128)S(1)} %get-tuple-element.20) | copy-start | bytes 6291460
  226.8 7.3 %collective-permute-start.4 = (f32[16,1,8,256]{3,0,2,1:T(8,128)S(1)}, f32[16,1,8,256]{3,0,2,1:T(8,128)S(1)}, u32[]{:S(2)}, u32[]{:S(2)}) collective-permute-start(f32[16,1,8,256]{3,0,2,1:T(8,128)S(1)} %get-tuple-element.234), channel_id=1, source_target_pairs={{16,0},{32,16},{48,32},{64,48},{80,64},{96,80},{112,96},{128,112},... | collective-permute-start | bytes 393224 | tf_op jit(solution)/shard_map/ppermute | solution.py:17
  231.6 7.1 %collective-permute-start.5 = (f32[16,1,8,256]{3,0,2,1:T(8,128)S(1)}, f32[16,1,8,256]{3,0,2,1:T(8,128)S(1)}, u32[]{:S(2)}, u32[]{:S(2)}) collective-permute-start(f32[16,1,8,256]{3,0,2,1:T(8,128)S(1)} %get-tuple-element.234), channel_id=1, source_target_pairs={{0,16},{16,32},{32,48},{48,64},{64,80},{80,96},{96,112},{112,128},... | collective-permute-start | bytes 393224 | tf_op jit(solution)/shard_map/ppermute | solution.py:16
  239.0 5.0 %collective-permute-start.6 = (f32[16,1,8,256]{3,0,2,1:T(8,128)S(1)}, f32[16,1,8,256]{3,0,2,1:T(8,128)S(1)}, u32[]{:S(2)}, u32[]{:S(2)}) collective-permute-start(f32[16,1,8,256]{3,0,2,1:T(8,128)S(1)} %get-tuple-element.12), channel_id=1, source_target_pairs={{16,0},{32,16},{48,32},{64,48},{80,64},{96,80},{112,96},{128,112},... | collective-permute-start | bytes 393224 | tf_op jit(solution)/shard_map/ppermute | solution.py:17
  239.1 7.2 %collective-permute-start.7 = (f32[16,1,8,256]{3,0,2,1:T(8,128)S(1)}, f32[16,1,8,256]{3,0,2,1:T(8,128)S(1)}, u32[]{:S(2)}, u32[]{:S(2)}) collective-permute-start(f32[16,1,8,256]{3,0,2,1:T(8,128)S(1)} %get-tuple-element.12), channel_id=1, source_target_pairs={{0,16},{16,32},{32,48},{48,64},{64,80},{80,96},{96,112},{112,128},... | collective-permute-start | bytes 393224 | tf_op jit(solution)/shard_map/ppermute | solution.py:16
  246.5 5.0 %collective-permute-start.8 = (f32[16,1,8,256]{3,0,2,1:T(8,128)S(1)}, f32[16,1,8,256]{3,0,2,1:T(8,128)S(1)}, u32[]{:S(2)}, u32[]{:S(2)}) collective-permute-start(f32[16,1,8,256]{3,0,2,1:T(8,128)S(1)} %get-tuple-element.10), channel_id=1, source_target_pairs={{16,0},{32,16},{48,32},{64,48},{80,64},{96,80},{112,96},{128,112},... | collective-permute-start | bytes 393224 | tf_op jit(solution)/shard_map/ppermute | solution.py:17
  246.6 7.2 %collective-permute-start.9 = (f32[16,1,8,256]{3,0,2,1:T(8,128)S(1)}, f32[16,1,8,256]{3,0,2,1:T(8,128)S(1)}, u32[]{:S(2)}, u32[]{:S(2)}) collective-permute-start(f32[16,1,8,256]{3,0,2,1:T(8,128)S(1)} %get-tuple-element.10), channel_id=1, source_target_pairs={{0,16},{16,32},{32,48},{48,64},{64,80},{80,96},{96,112},{112,128},... | collective-permute-start | bytes 393224 | tf_op jit(solution)/shard_map/ppermute | solution.py:16
  (75 other events, 212.9 us)
